TPU v7x, 32 devices: a whole 2x2x4 slice. The times are simulated.
32 devices in a mesh: wide: 8 (over y, x, core), narrow: 4 (over z).
Axes of the slice: x: 2, y: 2, z: 4, core: 2. Of those that a mesh axis runs over, the one named last changes fastest.
Arguments:
- states: bfloat16 [16384, 1024], P(('wide', 'narrow')), may hold values from -6 to 6
- applied: bfloat16 [16384, 1024], P(('wide', 'narrow')), may hold values from -6 to 6
- rotation: bfloat16 [2, 1024, 256], P(None, 'wide', 'narrow'), may hold values from -0.1875 to 0.1875
- ritz: float32 [2, 256], replicated, may hold values from 0.5 to 4
- potential: float32 [16384], P(('wide', 'narrow')), may hold values from 0.5 to 8
Outputs:
- rotated: bfloat16 [16384, 2, 256], P(('wide', 'narrow'))
- correction: bfloat16 [16384, 2, 256], P(('wide', 'narrow'))
- margin: float32 [2, 1024, 256], P(None, 'wide', 'narrow')
All inputs are finite; a program needn't handle non-finite values.
Results may differ from a plain program's by a relative error of at most 0.0095.
Values may be sent and summed in bfloat16 or wider, within the bound.
A program may use at most 64 MiB of HBM per device.

v0:
```python
import math

import jax
import jax.numpy as jnp
from jax import lax
from jax.sharding import PartitionSpec as P


def per_device(states, applied, rotation, ritz, potential):
    row_count = states.shape[0]
    total_rows = row_count * lax.axis_size("wide") * lax.axis_size("narrow")
    factor = 1.0 / math.sqrt(total_rows)
    contract = (((0,), (0,)), ((), ()))
    rotated_list = []
    correction_list = []
    margin_list = []
    for window in range(rotation.shape[0]):
        q_local = rotation[window]
        q_tall = lax.all_gather(q_local, "wide", axis=0, tiled=True)
        q_full = lax.all_gather(q_tall, "narrow", axis=1, tiled=True)
        plain = jnp.dot(states, q_full, preferred_element_type=jnp.float32)
        mapped = jnp.dot(applied, q_full, preferred_element_type=jnp.float32)
        eigen_values = ritz[window]
        residual = mapped - plain * eigen_values[None, :]
        fixed = (residual / (potential[:, None] + eigen_values[None, :])).astype(jnp.bfloat16)
        partial_value = lax.psum_scatter(
            lax.dot_general(states, fixed, contract, preferred_element_type=jnp.float32).astype(
                jnp.bfloat16
            ),
            "wide",
            scatter_dimension=0,
            tiled=True,
        )
        summed = lax.psum_scatter(partial_value, "narrow", scatter_dimension=1, tiled=True).astype(
            jnp.float32
        )
        rotated_list.append(plain.astype(jnp.bfloat16))
        correction_list.append(fixed)
        margin_list.append(summed * factor)
    return (
        jnp.stack(rotated_list, axis=1),
        jnp.stack(correction_list, axis=1),
        jnp.stack(margin_list, axis=0),
    )


def solution(mesh):
    placed = (
        P(("wide", "narrow"), None),
        P(("wide", "narrow"), None),
        P(None, "wide", "narrow"),
        P(),
        P(("wide", "narrow")),
    )
    return jax.shard_map(
        per_device,
        mesh=mesh,
        in_specs=placed,
        out_specs=(
            P(("wide", "narrow"), None, None),
            P(("wide", "narrow"), None, None),
            P(None, "wide", "narrow"),
        ),
        check_vma=False,
    )
```

profile of v0, /device:TPU:0, one launch (start us, length us, event | category | flops | bytes accessed | tf_op | source)
XLA Modules:
  0.0 160.5 jit_solution(8119105058409660867)
XLA Ops:
  7.2 0.8 fusion.13
  8.0 0.7 fusion.12
  8.7 10.5 %all-gather.2 = bf16[1,1024,64]{1,2,0:T(8,128)(2,1)S(1)} all-gather(bf16[1,128,64]{1,2,0:T(8,128)(2,1)S(1)} %get-tuple-element.10), channel_id=4, replica_groups=mesh['wide'=8,'narrow'=4] {'wide'}, dimensions={1}, use_global_device_ids=true | all-gather | bytes 147456 | tf_op jit(solution)/shard_map/all_gather | solution.py:19
  19.3 16.3 %all-gather.3 = bf16[1,1024,256]{1,2,0:T(8,128)(2,1)S(1)} all-gather(bf16[1,1024,64]{1,2,0:T(8,128)(2,1)S(1)} %all-gather.2), channel_id=5, replica_groups=mesh['wide'=8,'narrow'=4] {'narrow'}, dimensions={2}, use_global_device_ids=true | all-gather | bytes 655360 | tf_op jit(solution)/shard_map/all_gather | solution.py:20
  35.6 0.5 fusion.7
  36.1 0.7 copy-done.1
  36.8 0.5 fusion.4
  37.8 1.0 copy.14
  38.9 9.0 %all-gather = bf16[1,1024,64]{1,2,0:T(8,128)(2,1)S(1)} all-gather(bf16[1,128,64]{1,2,0:T(8,128)(2,1)S(1)} %get-tuple-element.9), channel_id=2, replica_groups=mesh['wide'=8,'narrow'=4] {'wide'}, dimensions={1}, use_global_device_ids=true | all-gather | bytes 147456 | tf_op jit(solution)/shard_map/all_gather | solution.py:19
  47.9 16.6 %all-gather.1 = bf16[1,1024,256]{1,2,0:T(8,128)(2,1)S(1)} all-gather(bf16[1,1024,64]{1,2,0:T(8,128)(2,1)S(1)} %all-gather), channel_id=3, replica_groups=mesh['wide'=8,'narrow'=4] {'narrow'}, dimensions={2}, use_global_device_ids=true | all-gather | bytes 655360 | tf_op jit(solution)/shard_map/all_gather | solution.py:20
  65.0 0.7 copy-done.2
  65.7 0.5 fusion.5
  66.6 1.0 copy.12
  67.8 5.8 %reduce-scatter.15.cloned.1.call-done = bf16[128,256]{1,0:T(8,128)(2,1)} async-done(((bf16[1024,256]{1,0:T(8,128)(2,1)}), bf16[128,256]{1,0:T(8,128)(2,1)}) %reduce-scatter.15.cloned.1.call-update) | async-done | bytes 65552
  73.6 1.6 copy.15
  75.3 1.3 copy.10
  76.7 1.3 copy.11
  78.0 32.8 %reduce-scatter.13.cloned.1.call-done = bf16[128,256]{1,0:T(8,128)(2,1)} async-done(((bf16[1024,256]{1,0:T(8,128)(2,1)}), bf16[128,256]{1,0:T(8,128)(2,1)}) %reduce-scatter.13.cloned.1.call-update) | async-done | bytes 65552
  110.9 1.6 copy.13
  112.5 20.6 %reduce-scatter.11.cloned.1.call-done = bf16[128,64]{0,1:T(8,128)(2,1)} async-done(((bf16[128,256]{0,1:T(8,128)(2,1)}), bf16[128,64]{0,1:T(8,128)(2,1)}) %reduce-scatter.11.cloned.1.call-update) | async-done | bytes 16400 | tf_op jit(solution)/shard_map/reduce_scatter | solution.py:34
  133.0 0.7 multiply_bitcast_fusion
  133.7 18.9 %reduce-scatter.9.cloned.1.call-done = bf16[128,64]{0,1:T(8,128)(2,1)} async-done(((bf16[128,256]{0,1:T(8,128)(2,1)}), bf16[128,64]{0,1:T(8,128)(2,1)}) %reduce-scatter.9.cloned.1.call-update) | async-done | bytes 16400 | tf_op jit(solution)/shard_map/reduce_scatter | solution.py:34
  152.6 0.7 multiply_bitcast_fusion.1
  153.3 0.6 pad_maximum_fusion.2
  (21 shorter events, 1.8 us)
Async XLA Ops:
  7.2 28.4 %copy-start = (bf16[512,1024]{1,0:T(8,128)(2,1)S(1)}, bf16[512,1024]{1,0:T(8,128)(2,1)}, u32[]{:S(2)}) copy-start(bf16[512,1024]{1,0:T(8,128)(2,1)} %param.5) | copy-start | bytes 3145732
  7.2 66.4 %reduce-scatter.15.cloned.1.call-start = ((), (), s32[]{:S(2)}) async-start(), calls=%async_computation.7 | async-start | bytes 589824
  35.6 1.2 copy-start.1
  36.1 0.7 copy-start.3
  38.8 72.1 %reduce-scatter.13.cloned.1.call-start = ((), (), s32[]{:S(2)}) async-start(), calls=%async_computation.6 | async-start | bytes 589824
  64.5 1.2 copy-start.2
  67.7 65.3 %reduce-scatter.11.cloned.1.call-start = ((), (), s32[]{:S(2)}) async-start(), calls=%async_computation.5 | async-start | bytes 81920 | tf_op jit(solution)/shard_map/reduce_scatter | solution.py:34
  75.2 77.4 %reduce-scatter.9.cloned.1.call-start = ((), (), s32[]{:S(2)}) async-start(), calls=%async_computation.4 | async-start | bytes 81920 | tf_op jit(solution)/shard_map/reduce_scatter | solution.py:34
Sparse Core Ops, SparseCore 0:
  38.9 34.6 reduce-scatter.14
  76.7 34.1 reduce-scatter.12
  113.7 19.2 reduce-scatter.10
  135.1 17.4 reduce-scatter.8
where the time goes:
time: 161 us; the launch traced here: 160 us
  waiting for transfers between devices  78.1 us (49%)
  blocking collectives  52.5 us (33%)
  between operations  13.9 us (9%)
  local copies, waits for them, and re-layouts  10.8 us (7%)
  matrix products  2.82 us (2%)
  other arithmetic  2.24 us (1%)
    reduce_scatter x2, waiting for transfers between devices, per_device(): lax.psum_scatter(partial_value, 'narrow', scatter_dimension=1, tiled=True)  39.4 us
    unnamed x6, waiting for transfers between devices  38.7 us
    all_gather x2, blocking collectives, per_device(): q_full = lax.all_gather(q_tall, 'narrow', axis=1, tiled=True)  32.9 us
    all_gather x2, blocking collectives, per_device(): q_tall = lax.all_gather(q_local, 'wide', axis=0, tiled=True)  19.6 us
    unnamed x14, local copies, waits for them, and re-layouts  9.3 us
  transfers between devices with their start and end apart: 4, of which 4 were waited for; matrix products, arithmetic and copies ran while one was open for 6% of the time, Pallas kernels for 0%

commit v1 on v0

v1 whole, which is shorter than its diff:
```python
import functools
import math

import jax
import jax.numpy as jnp
from jax import lax
from jax.experimental import pallas as pl
from jax.experimental.pallas import tpu as pltpu
from jax.sharding import PartitionSpec as P

F32 = jnp.float32
BF16 = jnp.bfloat16
CORE, XBIT, YBIT = 1, 2, 4


def flip(index, mask):
    out = index
    bit = 1
    while bit <= mask:
        if mask & bit:
            out = out + bit * (1 - 2 * ((index // bit) % 2))
        bit *= 2
    return out


def fused_kernel(
    factor, narrow,
    q_ref, ritz_ref, pot_ref, x_hbm, hx_hbm,
    rot_ref, cor_ref, mar_ref,
    x, hx, g, inv, p32, p16, a16, r1, r2, r3, f32s, f16, r4,
    in_sem, zs, zr, gs, gr, ds, dr, cs, cr, s1, t1, s2, t2, s3, t3, s4, t4,
):
    w = lax.axis_index("wide")
    n = lax.axis_index("narrow")
    blocks = q_ref.shape[0]
    wide_to = lambda mask: {"wide": flip(w, mask)}
    narrow_to = lambda d: {"narrow": flip(n, d)}
    sends = []

    def push(src, dst, send, recv, to):
        copy = pltpu.make_async_remote_copy(
            src_ref=src, dst_ref=dst, send_sem=send, recv_sem=recv,
            device_id=to, device_id_type=pl.DeviceIdType.MESH)
        copy.start()
        sends.append(copy)

    def arrived(dst, send, recv, to):
        pltpu.make_async_remote_copy(
            src_ref=dst, dst_ref=dst, send_sem=send, recv_sem=recv,
            device_id=to, device_id_type=pl.DeviceIdType.MESH).wait_recv()

    load_x = pltpu.make_async_copy(x_hbm, x, in_sem.at[0])
    load_hx = pltpu.make_async_copy(hx_hbm, hx, in_sem.at[1])
    load_x.start()
    load_hx.start()

    barrier = pltpu.get_barrier_semaphore()
    peers = [wide_to(m) for m in (CORE, XBIT, YBIT)] + [narrow_to(d) for d in range(1, narrow)]
    for peer in peers:
        pl.semaphore_signal(barrier, inc=1, device_id=peer, device_id_type=pl.DeviceIdType.MESH)
    pl.semaphore_wait(barrier, len(peers))

    wc, wx, wy, wd = (flip(w, m) for m in (CORE, XBIT, YBIT, XBIT | YBIT))
    near = (XBIT, YBIT, CORE)
    for d in range(1, narrow):
        push(q_ref, g.at[w, :, n], zs.at[d], zr.at[d], narrow_to(d))
    for i, m in enumerate(near):
        push(q_ref, g.at[w, :, n], gs.at[i, 0], gr.at[i, 0], wide_to(m))
    g[w, :, n] = q_ref[...]
    for d in range(1, narrow):
        nd = flip(n, d)
        arrived(g.at[w, :, nd], zs.at[d], zr.at[d], narrow_to(d))
        for i, m in enumerate(near):
            push(g.at[w, :, nd], g.at[w, :, nd], gs.at[i, d], gr.at[i, d], wide_to(m))

    pot_col = jnp.transpose(jnp.broadcast_to(pot_ref[...], (128, pot_ref.shape[1])))[:, :1]
    for k in range(blocks):
        inv[k] = 1.0 / (pot_col + ritz_ref[k : k + 1, :])

    for d in range(narrow):
        nd = flip(n, d)
        arrived(g.at[wx, :, nd], gs.at[0, d], gr.at[0, d], wide_to(XBIT))
        push(g.at[wx, 1, nd], g.at[wx, 1, nd], ds.at[1, d], dr.at[1, d], wide_to(YBIT))
        push(g.at[wx, :, nd], g.at[wx, :, nd], cs.at[0, d], cr.at[0, d], wide_to(CORE))
        arrived(g.at[wy, :, nd], gs.at[1, d], gr.at[1, d], wide_to(YBIT))
        push(g.at[wy, 0, nd], g.at[wy, 0, nd], ds.at[0, d], dr.at[0, d], wide_to(XBIT))
        push(g.at[wy, :, nd], g.at[wy, :, nd], cs.at[1, d], cr.at[1, d], wide_to(CORE))
    for d in range(narrow):
        nd = flip(n, d)
        for k, m in ((0, XBIT), (1, YBIT)):
            arrived(g.at[wd, k, nd], ds.at[k, d], dr.at[k, d], wide_to(m))
            push(g.at[wd, k, nd], g.at[wd, k, nd], cs.at[2 + k, d], cr.at[2 + k, d], wide_to(CORE))
    for d in range(narrow):
        nd = flip(n, d)
        arrived(g.at[wc, :, nd], gs.at[2, d], gr.at[2, d], wide_to(CORE))
        arrived(g.at[flip(wx, CORE), :, nd], cs.at[0, d], cr.at[0, d], wide_to(CORE))
        arrived(g.at[flip(wy, CORE), :, nd], cs.at[1, d], cr.at[1, d], wide_to(CORE))
        for k in range(2):
            arrived(g.at[flip(wd, CORE), k, nd], cs.at[2 + k, d], cr.at[2 + k, d], wide_to(CORE))
    load_x.wait()
    load_hx.wait()

    wide = g.shape[0]
    cols = g.shape[2] * g.shape[3]
    depth = g.shape[4]
    last = (((1,), (1,)), ((), ()))
    for k in range(blocks):
        q = jnp.concatenate([g[i, k].reshape(cols, depth) for i in range(wide)], axis=1)
        plain = lax.dot_general(x[...], q, last, preferred_element_type=F32)
        rot_ref[k] = plain.astype(BF16)
        mapped = lax.dot_general(hx[...], q, last, preferred_element_type=F32)
        cor_ref[k] = ((mapped - plain * ritz_ref[k : k + 1, :]) * inv[k]).astype(BF16)

    first = (((0,), (0,)), ((), ()))
    chip = w // 2
    core = w % 2
    block_shape = p16.shape[3:]
    order = (3, 1, 2, 0)
    for j in order:
        m = flip(chip, j)
        xc = x[:, pl.ds(pl.multiple_of(m * (2 * depth), 2 * depth), 2 * depth)]
        for k in range(blocks):
            part = lax.dot_general(cor_ref[k], xc, first, preferred_element_type=F32)
            for h in range(2):
                half = part[:, h * depth : (h + 1) * depth].reshape(block_shape)
                p32[j, h, k] = half
                p16[j, h, k] = half.astype(BF16)
        push(p16.at[j, 1 - core], r1.at[j], s1.at[j], t1.at[j], wide_to(CORE))

    lead = (XBIT, YBIT)
    for j in order:
        arrived(r1.at[j], s1.at[j], t1.at[j], wide_to(CORE))
        for k in range(2):
            total = p32[j, core, k] + r1[j, k].astype(F32)
            if j & (k + 1):
                a16[j, k] = total.astype(BF16)
                at = j ^ (k + 1)
                slot = 0 if at == 0 else 1
                push(a16.at[j, k], r2.at[k, slot], s2.at[k, slot], t2.at[k, slot], wide_to(lead[k]))
            else:
                p32[j, core, k] = total
    for k in range(2):
        j = 2 - k
        arrived(r2.at[k, 1], s2.at[k, 1], t2.at[k, 1], wide_to(lead[k]))
        a16[j, k] = (p32[j, core, k] + r2[k, 1].astype(F32)).astype(BF16)
        push(a16.at[j, k], r3.at[k], s3.at[k], t3.at[k], wide_to(lead[1 - k]))
    for k in range(2):
        arrived(r2.at[k, 0], s2.at[k, 0], t2.at[k, 0], wide_to(lead[k]))
        arrived(r3.at[k], s3.at[k], t3.at[k], wide_to(lead[1 - k]))
        total = p32[0, core, k] + r2[k, 0].astype(F32) + r3[k].astype(F32)
        f32s[k] = total
        f16[k] = total.astype(BF16)
    for d in range(1, narrow):
        push(f16.at[:, flip(n, d)], r4.at[d], s4.at[d], t4.at[d], narrow_to(d))
    out = f32s[:, n]
    for d in range(1, narrow):
        arrived(r4.at[d], s4.at[d], t4.at[d], narrow_to(d))
        out = out + r4[d].astype(F32)
    mar_ref[...] = out * factor
    for copy in sends:
        copy.wait_send()


def fused(wide, narrow, states, applied, rotation, ritz, potential):
    rows, nst = states.shape
    blocks, depth, part = rotation.shape
    cols = part * narrow
    factor = 1.0 / math.sqrt(rows * wide * narrow)
    dma = pltpu.SemaphoreType.DMA
    vmem = pl.BlockSpec(memory_space=pltpu.VMEM)
    hbm = pl.BlockSpec(memory_space=pltpu.HBM)
    tile = (narrow, part, depth)
    chips = wide // 2
    rot, cor, mar = pl.pallas_call(
        functools.partial(fused_kernel, factor, narrow),
        out_shape=(
            jax.ShapeDtypeStruct((blocks, rows, cols), BF16),
            jax.ShapeDtypeStruct((blocks, rows, cols), BF16),
            jax.ShapeDtypeStruct((blocks, part, depth), F32),
        ),
        in_specs=[vmem, vmem, vmem, hbm, hbm],
        out_specs=(vmem, vmem, vmem),
        scratch_shapes=[
            pltpu.VMEM((rows, nst), BF16),
            pltpu.VMEM((rows, nst), BF16),
            pltpu.VMEM((wide, blocks) + tile, BF16),
            pltpu.VMEM((blocks, rows, cols), F32),
            pltpu.VMEM((chips, 2, blocks) + tile, F32),
            pltpu.VMEM((chips, 2, blocks) + tile, BF16),
            pltpu.VMEM((chips, blocks) + tile, BF16),
            pltpu.VMEM((chips, blocks) + tile, BF16),
            pltpu.VMEM((blocks, 2) + tile, BF16),
            pltpu.VMEM((blocks,) + tile, BF16),
            pltpu.VMEM((blocks,) + tile, F32),
            pltpu.VMEM((blocks,) + tile, BF16),
            pltpu.VMEM((narrow, blocks, part, depth), BF16),
            dma((2,)),
            dma((narrow,)), dma((narrow,)),
            dma((3, narrow)), dma((3, narrow)),
            dma((2, narrow)), dma((2, narrow)),
            dma((4, narrow)), dma((4, narrow)),
            dma((chips,)), dma((chips,)),
            dma((2, 2)), dma((2, 2)),
            dma((2,)), dma((2,)),
            dma((narrow,)), dma((narrow,)),
        ],
        compiler_params=pltpu.CompilerParams(
            collective_id=0, has_side_effects=True, vmem_limit_bytes=40 * 1024 * 1024),
    )(jnp.swapaxes(rotation, 1, 2), ritz, potential.reshape(1, rows), states, applied)
    return (
        jnp.swapaxes(rot, 0, 1),
        jnp.swapaxes(cor, 0, 1),
        jnp.swapaxes(mar, 1, 2),
    )


def plain_path(states, applied, rotation, ritz, potential):
    row_count = states.shape[0]
    total_rows = row_count * lax.axis_size("wide") * lax.axis_size("narrow")
    factor = 1.0 / math.sqrt(total_rows)
    contract = (((0,), (0,)), ((), ()))
    rotated_list = []
    correction_list = []
    margin_list = []
    for window in range(rotation.shape[0]):
        q_local = rotation[window]
        q_tall = lax.all_gather(q_local, "wide", axis=0, tiled=True)
        q_full = lax.all_gather(q_tall, "narrow", axis=1, tiled=True)
        plain = jnp.dot(states, q_full, preferred_element_type=F32)
        mapped = jnp.dot(applied, q_full, preferred_element_type=F32)
        eigen_values = ritz[window]
        residual = mapped - plain * eigen_values[None, :]
        fixed = (residual / (potential[:, None] + eigen_values[None, :])).astype(BF16)
        partial_value = lax.psum_scatter(
            lax.dot_general(states, fixed, contract, preferred_element_type=F32).astype(BF16),
            "wide",
            scatter_dimension=0,
            tiled=True,
        )
        summed = lax.psum_scatter(partial_value, "narrow", scatter_dimension=1, tiled=True).astype(F32)
        rotated_list.append(plain.astype(BF16))
        correction_list.append(fixed)
        margin_list.append(summed * factor)
    return (
        jnp.stack(rotated_list, axis=1),
        jnp.stack(correction_list, axis=1),
        jnp.stack(margin_list, axis=0),
    )


def solution(mesh):
    wide, narrow = mesh.shape["wide"], mesh.shape["narrow"]

    def per_device(states, applied, rotation, ritz, potential):
        blocks, depth, part = rotation.shape
        fits = (
            wide == 1 << 3 and narrow & (narrow - 1) == 0 and blocks == 2
            and depth % 128 == 0 and part % 16 == 0 and states.shape[0] % 128 == 0
        )
        if fits:
            return fused(wide, narrow, states, applied, rotation, ritz, potential)
        return plain_path(states, applied, rotation, ritz, potential)

    placed = (
        P(("wide", "narrow"), None),
        P(("wide", "narrow"), None),
        P(None, "wide", "narrow"),
        P(),
        P(("wide", "narrow")),
    )
    return jax.shard_map(
        per_device,
        mesh=mesh,
        in_specs=placed,
        out_specs=(
            P(("wide", "narrow"), None, None),
            P(("wide", "narrow"), None, None),
            P(None, "wide", "narrow"),
        ),
        check_vma=False,
    )
```

time: 161 us -> 41.7 us (0.26)
  waiting for transfers between devices: 78.1 us -> 0 us
  blocking collectives: 52.5 us -> 0 us
  Pallas kernels: 0 us -> 32.8 us
  between operations: 13.9 us -> 0.65 us
  local copies, waits for them, and re-layouts: 10.8 us -> 7.86 us
  matrix products: 2.82 us -> 0 us
  other arithmetic: 2.24 us -> 0 us
    all_gather x4 -> x0, blocking collectives: 52.5 us -> none  [the longest x2 32.9 us: per_device(): q_full = lax.all_gather(q_tall, 'narrow', axis=1, tiled=True)]
    reduce_scatter x2 -> x0, waiting for transfers between devices: 39.4 us -> none  [per_device(): lax.psum_scatter(partial_value, 'narrow', scatter_dimension=1, tiled=True)]
    unnamed x6 -> x0, waiting for transfers between devices: 38.7 us -> none
    pallas_call x0 -> x1, Pallas kernels: none -> 32.8 us  [fused(): pl.pallas_call(functools.partial(fused_kernel, factor, narrow), out_shape...]
    dot_general x6 -> x0, matrix products: 2.82 us -> none  [the longest x2 0.95 us: per_device(): mapped = jnp.dot(applied, q_full, preferred_element_type=jnp.float32)]
    another operation x7 -> x0, other arithmetic: 2.24 us -> none  [the longest x3 2.08 us: per_device(): jnp.stack(margin_list, axis=0)]
    unnamed x14 -> x13, local copies, waits for them, and re-layouts: 9.3 us -> 7.86 us
  transfers between devices with their start and end apart: 4 -> 0, of which waited for: 4 -> 0; matrix products, arithmetic and copies ran while one was open for 6% -> 0% of each run, Pallas kernels for 0% -> 0%
where the time goes in v1:
time: 41.7 us; the launch traced here: 41.4 us
  Pallas kernels  32.8 us (79%)
  local copies, waits for them, and re-layouts  7.86 us (19%)
  between operations  0.65 us (2%)
    pallas_call x1, Pallas kernels, fused(): pl.pallas_call(functools.partial(fused_kernel, factor, narrow), out_shape...  32.8 us
    unnamed x13, local copies, waits for them, and re-layouts  7.86 us

profile of v1, /device:TPU:0, one launch (start us, length us, event | category | flops | bytes accessed | tf_op | source)
XLA Modules:
  0.0 41.4 jit_solution(10164788159921590641)
XLA Ops:
  0.6 0.0 copy-start.3
  0.6 0.7 %copy-done.3 = f32[2,256]{1,0:T(2,128)S(1)} copy-done((f32[2,256]{1,0:T(2,128)S(1)}, f32[2,256]{1,0:T(2,128)}, u32[]{:S(2)}) %copy-start.3) | copy-done | bytes 2072
  1.3 0.0 copy-start
  1.3 1.2 %copy-done = bf16[512,1024]{1,0:T(8,128)(2,1)S(1)} copy-done((bf16[512,1024]{1,0:T(8,128)(2,1)S(1)}, bf16[512,1024]{1,0:T(8,128)(2,1)}, u32[]{:S(2)}) %copy-start) | copy-done | bytes 1048600
  2.5 0.0 copy-start.1
  2.5 1.2 %copy-done.1 = bf16[512,1024]{1,0:T(8,128)(2,1)S(1)} copy-done((bf16[512,1024]{1,0:T(8,128)(2,1)S(1)}, bf16[512,1024]{1,0:T(8,128)(2,1)}, u32[]{:S(2)}) %copy-start.1) | copy-done | bytes 1048600
  3.8 0.0 copy-start.2
  3.8 0.8 %copy-done.2 = bf16[2,128,64]{1,2,0:T(8,128)(2,1)S(1)} copy-done((bf16[2,128,64]{1,2,0:T(8,128)(2,1)S(1)}, bf16[2,128,64]{1,2,0:T(8,128)(2,1)}, u32[]{:S(2)}) %copy-start.2) | copy-done | bytes 32792
  4.5 0.0 copy-start.4
  4.5 0.7 %copy-done.4 = f32[512]{0:T(512)S(1)} copy-done((f32[512]{0:T(512)S(1)}, f32[512]{0:T(512)}, u32[]{:S(2)}) %copy-start.4) | copy-done | bytes 2072
  5.2 32.8 %shard_map.76 = (bf16[2,512,256]{2,1,0:T(8,128)(2,1)S(1)}, bf16[2,512,256]{2,1,0:T(8,128)(2,1)S(1)}, f32[2,64,128]{2,1,0:T(8,128)S(1)}) custom-call(bf16[2,64,128]{2,1,0:T(8,128)(2,1)S(1)} %bitcast.8, f32[2,256]{1,0:T(2,128)S(1)} %copy-done.3, f32[1,512]{1,0:T(1,128)S(1)} %bitcast.9, bf16[512,1024]{1,0:T(8,128)(2,1)S(1)} %copy-done, ...), custom_call_target="tpu_custom_call" | custom-call | tf_op jit(solution)/shard_map/pallas_call | solution.py:174
  38.1 1.3 %copy.8 = bf16[512,2,256]{2,1,0:T(2,128)(2,1)} copy(bf16[512,2,256]{2,0,1:T(8,128)(2,1)S(1)} %bitcast.6) | data formatting | bytes 1048576
  39.4 1.3 %copy.9 = bf16[512,2,256]{2,1,0:T(2,128)(2,1)} copy(bf16[512,2,256]{2,0,1:T(8,128)(2,1)S(1)} %bitcast.5) | data formatting | bytes 1048576
  40.7 0.6 %copy.11 = f32[2,128,64]{1,2,0:T(8,128)} copy(f32[2,128,64]{1,2,0:T(8,128)S(1)} %bitcast.7) | data formatting | bytes 131072
Async XLA Ops:
  0.6 0.7 %copy-start.3 = (f32[2,256]{1,0:T(2,128)S(1)}, f32[2,256]{1,0:T(2,128)}, u32[]{:S(2)}) copy-start(f32[2,256]{1,0:T(2,128)} %ritz_ref.1) | copy-start | bytes 6148
  1.3 1.2 %copy-start = (bf16[512,1024]{1,0:T(8,128)(2,1)S(1)}, bf16[512,1024]{1,0:T(8,128)(2,1)}, u32[]{:S(2)}) copy-start(bf16[512,1024]{1,0:T(8,128)(2,1)} %x_hbm.1) | copy-start | bytes 3145732
  2.5 1.2 %copy-start.1 = (bf16[512,1024]{1,0:T(8,128)(2,1)S(1)}, bf16[512,1024]{1,0:T(8,128)(2,1)}, u32[]{:S(2)}) copy-start(bf16[512,1024]{1,0:T(8,128)(2,1)} %hx_hbm.1) | copy-start | bytes 3145732
  3.8 0.8 %copy-start.2 = (bf16[2,128,64]{1,2,0:T(8,128)(2,1)S(1)}, bf16[2,128,64]{1,2,0:T(8,128)(2,1)}, u32[]{:S(2)}) copy-start(bf16[2,128,64]{1,2,0:T(8,128)(2,1)} %param.7) | copy-start | bytes 98308
  4.5 0.7 %copy-start.4 = (f32[512]{0:T(512)S(1)}, f32[512]{0:T(512)}, u32[]{:S(2)}) copy-start(f32[512]{0:T(512)} %param.9) | copy-start | bytes 6148

commit v2 on v1

v2 whole, which is shorter than its diff:
```python
import functools
import math

import jax
import jax.numpy as jnp
from jax import lax
from jax.experimental import pallas as pl
from jax.experimental.pallas import tpu as pltpu
from jax.sharding import PartitionSpec as P

F32 = jnp.float32
BF16 = jnp.bfloat16
CORE, XBIT, YBIT = 1, 2, 4


def flip(index, mask):
    out = index
    bit = 1
    while bit <= mask:
        if mask & bit:
            out = out + bit * (1 - 2 * ((index // bit) % 2))
        bit *= 2
    return out


def fused_kernel(
    factor, narrow,
    q_hbm, ritz_hbm, pot_hbm, x_hbm, hx_hbm,
    rot_hbm, cor_hbm, mar_ref,
    rot_ref, cor_ref, rot_out, cor_out, out_sem, q_ref, ritz_ref, pot_ref, x, hx, g, inv, p32, p16, a16, r1, r2, f16, r4,
    in_sem, zs, zr, gs, gr, cs, cr, s1, t1, s2, t2, s4, t4,
):
    w = lax.axis_index("wide")
    n = lax.axis_index("narrow")
    blocks = q_ref.shape[0]
    loads = [
        pltpu.make_async_copy(src, dst, in_sem.at[i])
        for i, (src, dst) in enumerate(
            ((q_hbm, q_ref), (ritz_hbm, ritz_ref), (pot_hbm, pot_ref), (x_hbm, x), (hx_hbm, hx)))
    ]
    for load in loads:
        load.start()
    wide_to = lambda mask: {"wide": flip(w, mask)}
    narrow_to = lambda d: {"narrow": flip(n, d)}
    sends = []

    def push(src, dst, send, recv, to):
        copy = pltpu.make_async_remote_copy(
            src_ref=src, dst_ref=dst, send_sem=send, recv_sem=recv,
            device_id=to, device_id_type=pl.DeviceIdType.MESH)
        copy.start()
        sends.append(copy)

    def arrived(dst, send, recv, to):
        pltpu.make_async_remote_copy(
            src_ref=dst, dst_ref=dst, send_sem=send, recv_sem=recv,
            device_id=to, device_id_type=pl.DeviceIdType.MESH).wait_recv()

    barrier = pltpu.get_barrier_semaphore()
    peers = [wide_to(m) for m in (CORE, XBIT, YBIT, XBIT | YBIT)] + [narrow_to(d) for d in range(1, narrow)]
    for peer in peers:
        pl.semaphore_signal(barrier, inc=1, device_id=peer, device_id_type=pl.DeviceIdType.MESH)
    loads[0].wait()
    pl.semaphore_wait(barrier, len(peers))

    near = (XBIT | YBIT, XBIT, YBIT)
    for d in range(narrow - 1, 0, -1):
        push(q_ref, g.at[w, :, n], zs.at[d], zr.at[d], narrow_to(d))
    for i, m in enumerate(near + (CORE,)):
        push(q_ref, g.at[w, :, n], gs.at[i, 0], gr.at[i, 0], wide_to(m))
    g[w, :, n] = q_ref[...]
    for d in range(1, narrow):
        nd = flip(n, d)
        arrived(g.at[w, :, nd], zs.at[d], zr.at[d], narrow_to(d))
        for i, m in enumerate(near + (CORE,)):
            push(g.at[w, :, nd], g.at[w, :, nd], gs.at[i, d], gr.at[i, d], wide_to(m))

    loads[1].wait()
    loads[2].wait()
    pot_col = jnp.transpose(jnp.broadcast_to(pot_ref[...], (128, pot_ref.shape[1])))[:, :1]
    for k in range(blocks):
        inv[k] = 1.0 / (pot_col + ritz_ref[k : k + 1, :])

    for d in range(narrow):
        nd = flip(n, d)
        for i, m in enumerate(near):
            wm = flip(w, m)
            arrived(g.at[wm, :, nd], gs.at[i, d], gr.at[i, d], wide_to(m))
            push(g.at[wm, :, nd], g.at[wm, :, nd], cs.at[i, d], cr.at[i, d], wide_to(CORE))
    for d in range(narrow):
        nd = flip(n, d)
        arrived(g.at[flip(w, CORE), :, nd], gs.at[3, d], gr.at[3, d], wide_to(CORE))
        for i, m in enumerate(near):
            arrived(g.at[flip(w, m | CORE), :, nd], cs.at[i, d], cr.at[i, d], wide_to(CORE))
    loads[3].wait()
    loads[4].wait()

    wide = g.shape[0]
    cols = g.shape[2] * g.shape[3]
    depth = g.shape[4]
    last = (((1,), (1,)), ((), ()))
    for k in range(blocks):
        q = jnp.concatenate([g[i, k].reshape(cols, depth) for i in range(wide)], axis=1)
        plain = lax.dot_general(x[...], q, last, preferred_element_type=F32)
        rot_ref[k] = plain
        mapped = lax.dot_general(hx[...], q, last, preferred_element_type=F32)
        cor_ref[k] = ((mapped - plain * ritz_ref[k : k + 1, :]) * inv[k]).astype(BF16)

    first = (((0,), (0,)), ((), ()))
    chips = wide // 2
    chip = w // 2
    core = w % 2
    for m in range(chips):
        xc = x[:, 2 * m * depth : 2 * (m + 1) * depth]
        for k in range(blocks):
            part = lax.dot_general(cor_ref[k], xc, first, preferred_element_type=F32)
            for h in range(2):
                half = part[:, h * depth : (h + 1) * depth].reshape(g.shape[2:])
                p32[h, :, m, k] = half
                p16[h, :, m, k] = half.astype(BF16)
    away = range(narrow - 1, -1, -1)
    for d in away:
        push(p16.at[1 - core, flip(n, d)], r1.at[d], s1.at[d], t1.at[d], wide_to(CORE))
    for d in away:
        nd = flip(n, d)
        arrived(r1.at[d], s1.at[d], t1.at[d], wide_to(CORE))
        for i, m in enumerate(near):
            j = flip(chip, m // 2)
            a16[d, i] = (p32[core, nd, j] + r1[d, j].astype(F32)).astype(BF16)
            push(a16.at[d, i], r2.at[d, i], s2.at[d, i], t2.at[d, i], wide_to(m))
    outs = []
    for i, (src, dst, dst_hbm) in enumerate(((rot_ref, rot_out, rot_hbm), (cor_ref, cor_out, cor_hbm))):
        dst[...] = jnp.stack([src[k].astype(F32) for k in range(blocks)], axis=1).astype(BF16)
        out = pltpu.make_async_copy(dst, dst_hbm, out_sem.at[i])
        out.start()
        outs.append(out)
    for d in away:
        total = p32[core, flip(n, d), chip] + r1[d, chip].astype(F32)
        for i, m in enumerate(near):
            arrived(r2.at[d, i], s2.at[d, i], t2.at[d, i], wide_to(m))
            total = total + r2[d, i].astype(F32)
        if d > 0:
            f16[d] = total.astype(BF16)
            push(f16.at[d], r4.at[d], s4.at[d], t4.at[d], narrow_to(d))
    for d in away[:-1]:
        arrived(r4.at[d], s4.at[d], t4.at[d], narrow_to(d))
        total = total + r4[d].astype(F32)
    mar_ref[...] = total * factor
    for out in outs:
        out.wait()
    for copy in sends:
        copy.wait_send()


def hand_over_kernel(cuts, *refs):
    count = len(cuts)
    sources, targets, held = refs[:count], refs[count : 2 * count], refs[2 * count : 3 * count]
    in_sem, out_sem = refs[3 * count :]
    pieces = []
    for a, pieces_of in enumerate(cuts):
        size = sources[a].shape[0] // pieces_of
        pieces += [(a, pl.ds(i * size, size)) for i in range(pieces_of)]
    reads = [
        pltpu.make_async_copy(sources[a].at[cut], held[a].at[cut], in_sem.at[i])
        for i, (a, cut) in enumerate(pieces)
    ]
    writes = [
        pltpu.make_async_copy(held[a].at[cut], targets[a].at[cut], out_sem.at[i])
        for i, (a, cut) in enumerate(pieces)
    ]
    for read in reads:
        read.start()
    for read, write in zip(reads, writes):
        read.wait()
        write.start()
    for write in writes:
        write.wait()


def hand_over(arrays, cuts):
    hbm = pl.BlockSpec(memory_space=pltpu.HBM)
    return pl.pallas_call(
        functools.partial(hand_over_kernel, cuts),
        out_shape=tuple(jax.ShapeDtypeStruct(a.shape, a.dtype) for a in arrays),
        in_specs=[hbm] * len(arrays),
        out_specs=(hbm,) * len(arrays),
        scratch_shapes=[pltpu.VMEM(a.shape, a.dtype) for a in arrays]
        + [pltpu.SemaphoreType.DMA((sum(cuts),))] * 2,
        compiler_params=pltpu.CompilerParams(vmem_limit_bytes=60 * 1024 * 1024),
    )(*arrays)


def fused(wide, narrow, states, applied, rotation, ritz, potential):
    rows, nst = states.shape
    blocks, depth, part = rotation.shape
    cols = part * narrow
    factor = 1.0 / math.sqrt(rows * wide * narrow)
    dma = pltpu.SemaphoreType.DMA
    vmem = pl.BlockSpec(memory_space=pltpu.VMEM)
    hbm = pl.BlockSpec(memory_space=pltpu.HBM)
    tile = (narrow, part, depth)
    tile_in = (blocks, part, depth)
    chips = wide // 2
    rot, cor, mar = pl.pallas_call(
        functools.partial(fused_kernel, factor, narrow),
        out_shape=(
            jax.ShapeDtypeStruct((rows, blocks, cols), BF16),
            jax.ShapeDtypeStruct((rows, blocks, cols), BF16),
            jax.ShapeDtypeStruct((blocks, part, depth), F32),
        ),
        in_specs=[hbm] * 5,
        out_specs=(hbm, hbm, vmem),
        scratch_shapes=[
            pltpu.VMEM((blocks, rows, cols), F32),
            pltpu.VMEM((blocks, rows, cols), BF16),
            pltpu.VMEM((rows, blocks, cols), BF16),
            pltpu.VMEM((rows, blocks, cols), BF16),
            dma((2,)),
            pltpu.VMEM(tile_in, BF16),
            pltpu.VMEM(ritz.shape, F32),
            pltpu.VMEM((1, rows), F32),
            pltpu.VMEM((rows, nst), BF16),
            pltpu.VMEM((rows, nst), BF16),
            pltpu.VMEM((wide, blocks) + tile, BF16),
            pltpu.VMEM((blocks, rows, cols), F32),
            pltpu.VMEM((2, narrow, chips) + tile_in, F32),
            pltpu.VMEM((2, narrow, chips) + tile_in, BF16),
            pltpu.VMEM((narrow, 3) + tile_in, BF16),
            pltpu.VMEM((narrow, chips) + tile_in, BF16),
            pltpu.VMEM((narrow, 3) + tile_in, BF16),
            pltpu.VMEM((narrow,) + tile_in, BF16),
            pltpu.VMEM((narrow,) + tile_in, BF16),
            dma((5,)),
            dma((narrow,)), dma((narrow,)),
            dma((4, narrow)), dma((4, narrow)),
            dma((3, narrow)), dma((3, narrow)),
            dma((narrow,)), dma((narrow,)),
            dma((narrow, 3)), dma((narrow, 3)),
            dma((narrow,)), dma((narrow,)),
        ],
        compiler_params=pltpu.CompilerParams(
            collective_id=0, has_side_effects=True, vmem_limit_bytes=60 * 1024 * 1024),
    )(jnp.swapaxes(rotation, 1, 2), ritz, potential.reshape(1, rows), states, applied)
    rot, cor, mar = hand_over((rot, cor, mar), (2, 2, 1))
    return (
        rot,
        cor,
        jnp.swapaxes(mar, 1, 2),
    )


def plain_path(states, applied, rotation, ritz, potential):
    row_count = states.shape[0]
    total_rows = row_count * lax.axis_size("wide") * lax.axis_size("narrow")
    factor = 1.0 / math.sqrt(total_rows)
    contract = (((0,), (0,)), ((), ()))
    rotated_list = []
    correction_list = []
    margin_list = []
    for window in range(rotation.shape[0]):
        q_local = rotation[window]
        q_tall = lax.all_gather(q_local, "wide", axis=0, tiled=True)
        q_full = lax.all_gather(q_tall, "narrow", axis=1, tiled=True)
        plain = jnp.dot(states, q_full, preferred_element_type=F32)
        mapped = jnp.dot(applied, q_full, preferred_element_type=F32)
        eigen_values = ritz[window]
        residual = mapped - plain * eigen_values[None, :]
        fixed = (residual / (potential[:, None] + eigen_values[None, :])).astype(BF16)
        partial_value = lax.psum_scatter(
            lax.dot_general(states, fixed, contract, preferred_element_type=F32).astype(BF16),
            "wide",
            scatter_dimension=0,
            tiled=True,
        )
        summed = lax.psum_scatter(partial_value, "narrow", scatter_dimension=1, tiled=True).astype(F32)
        rotated_list.append(plain.astype(BF16))
        correction_list.append(fixed)
        margin_list.append(summed * factor)
    return (
        jnp.stack(rotated_list, axis=1),
        jnp.stack(correction_list, axis=1),
        jnp.stack(margin_list, axis=0),
    )


def solution(mesh):
    wide, narrow = mesh.shape["wide"], mesh.shape["narrow"]

    def per_device(states, applied, rotation, ritz, potential):
        blocks, depth, part = rotation.shape
        fits = (
            wide == 1 << 3 and narrow & (narrow - 1) == 0 and blocks == 2
            and depth % 128 == 0 and part % 16 == 0 and states.shape[0] % 128 == 0
        )
        if fits:
            return fused(wide, narrow, states, applied, rotation, ritz, potential)
        return plain_path(states, applied, rotation, ritz, potential)

    placed = (
        P(("wide", "narrow"), None),
        P(("wide", "narrow"), None),
        P(None, "wide", "narrow"),
        P(),
        P(("wide", "narrow")),
    )
    return jax.shard_map(
        per_device,
        mesh=mesh,
        in_specs=placed,
        out_specs=(
            P(("wide", "narrow"), None, None),
            P(("wide", "narrow"), None, None),
            P(None, "wide", "narrow"),
        ),
        check_vma=False,
    )
```

time: 41.7 us -> 32.3 us (0.77)
  local copies, waits for them, and re-layouts: 7.86 us -> 0 us
  Pallas kernels: 32.8 us -> 31.5 us
    unnamed x13 -> x0, local copies, waits for them, and re-layouts: 7.86 us -> none
    pallas_call x1, Pallas kernels: 32.8 us -> 29.5 us  [fused(): pl.pallas_call(functools.partial(fused_kernel, factor, narrow), out_shape...]
    pallas_call x0 -> x1, Pallas kernels: none -> 2.01 us  [hand_over(): pl.pallas_call(functools.partial(hand_over_kernel, cuts), out_shape=tuple...]
where the time goes in v2:
time: 32.3 us; the launch traced here: 32.2 us
  Pallas kernels  31.5 us (98%)
  between operations  0.64 us (2%)
    pallas_call x1, Pallas kernels, fused(): pl.pallas_call(functools.partial(fused_kernel, factor, narrow), out_shape...  29.5 us
    pallas_call x1, Pallas kernels, hand_over(): pl.pallas_call(functools.partial(hand_over_kernel, cuts), out_shape=tuple...  2.01 us

profile of v2, /device:TPU:0, one launch (start us, length us, event | category | flops | bytes accessed | tf_op | source)
XLA Modules:
  0.0 32.2 jit_solution(9736411205275958218)
XLA Ops:
  0.6 29.5 %shard_map.76 = (bf16[512,2,256]{2,1,0:T(2,128)(2,1)}, bf16[512,2,256]{2,1,0:T(2,128)(2,1)}, f32[2,64,128]{2,1,0:T(8,128)}) custom-call(bf16[2,64,128]{2,1,0:T(8,128)(2,1)} %bitcast.3, f32[2,256]{1,0:T(2,128)} %ritz_hbm.1, f32[1,512]{1,0:T(1,128)} %bitcast.4, bf16[512,1024]{1,0:T(8,128)(2,1)} %x_hbm.1, bf16[512,1024]{1,0:T(8,128)(2,1)} %hx_hbm.1), custom_call_target="tpu_custom_call" | custom-call | tf_op jit(solution)/shard_map/pallas_call | solution.py:204
  30.2 2.0 %shard_map.77 = (bf16[512,2,256]{2,1,0:T(2,128)(2,1)}, bf16[512,2,256]{2,1,0:T(2,128)(2,1)}, f32[2,64,128]{2,1,0:T(8,128)}) custom-call(bf16[512,2,256]{2,1,0:T(2,128)(2,1)} %get-tuple-element.9.refs_0_, bf16[512,2,256]{2,1,0:T(2,128)(2,1)} %get-tuple-element.10.refs_1_, f32[2,64,128]{2,1,0:T(8,128)} %get-tuple-element.11.refs_2_), custom_call_target="tpu_custom_call" | custom-call | tf_op jit(solution)/shard_map/pallas_call | solution.py:182

commit v3 on v2

--- a/solution.py
+++ b/solution.py
@@ -64,16 +64,18 @@
     pl.semaphore_wait(barrier, len(peers))
 
     near = (XBIT | YBIT, XBIT, YBIT)
-    for d in range(narrow - 1, 0, -1):
-        push(q_ref, g.at[w, :, n], zs.at[d], zr.at[d], narrow_to(d))
-    for i, m in enumerate(near + (CORE,)):
-        push(q_ref, g.at[w, :, n], gs.at[i, 0], gr.at[i, 0], wide_to(m))
-    g[w, :, n] = q_ref[...]
-    for d in range(1, narrow):
-        nd = flip(n, d)
-        arrived(g.at[w, :, nd], zs.at[d], zr.at[d], narrow_to(d))
+    for k in range(blocks):
+        for d in range(narrow - 1, 0, -1):
+            push(q_ref.at[k], g.at[k, w, n], zs.at[k, d], zr.at[k, d], narrow_to(d))
         for i, m in enumerate(near + (CORE,)):
-            push(g.at[w, :, nd], g.at[w, :, nd], gs.at[i, d], gr.at[i, d], wide_to(m))
+            push(q_ref.at[k], g.at[k, w, n], gs.at[k, i, 0], gr.at[k, i, 0], wide_to(m))
+        g[k, w, n] = q_ref[k]
+    for k in range(blocks):
+        for d in range(1, narrow):
+            own = g.at[k, w, flip(n, d)]
+            arrived(own, zs.at[k, d], zr.at[k, d], narrow_to(d))
+            for i, m in enumerate(near + (CORE,)):
+                push(own, own, gs.at[k, i, d], gr.at[k, i, d], wide_to(m))
 
     loads[1].wait()
     loads[2].wait()
@@ -81,71 +83,93 @@
     for k in range(blocks):
         inv[k] = 1.0 / (pot_col + ritz_ref[k : k + 1, :])
 
-    for d in range(narrow):
-        nd = flip(n, d)
-        for i, m in enumerate(near):
-            wm = flip(w, m)
-            arrived(g.at[wm, :, nd], gs.at[i, d], gr.at[i, d], wide_to(m))
-            push(g.at[wm, :, nd], g.at[wm, :, nd], cs.at[i, d], cr.at[i, d], wide_to(CORE))
-    for d in range(narrow):
-        nd = flip(n, d)
-        arrived(g.at[flip(w, CORE), :, nd], gs.at[3, d], gr.at[3, d], wide_to(CORE))
-        for i, m in enumerate(near):
-            arrived(g.at[flip(w, m | CORE), :, nd], cs.at[i, d], cr.at[i, d], wide_to(CORE))
-    loads[3].wait()
-    loads[4].wait()
-
-    wide = g.shape[0]
+    def pass_on(k):
+        for d in range(narrow):
+            for i, m in enumerate(near):
+                block = g.at[k, flip(w, m), flip(n, d)]
+                arrived(block, gs.at[k, i, d], gr.at[k, i, d], wide_to(m))
+                push(block, block, cs.at[k, i, d], cr.at[k, i, d], wide_to(CORE))
+
+    def gathered(k):
+        for d in range(narrow):
+            nd = flip(n, d)
+            arrived(g.at[k, flip(w, CORE), nd], gs.at[k, 3, d], gr.at[k, 3, d], wide_to(CORE))
+            for i, m in enumerate(near):
+                arrived(g.at[k, flip(w, m | CORE), nd], cs.at[k, i, d], cr.at[k, i, d], wide_to(CORE))
+
+    wide = g.shape[1]
     cols = g.shape[2] * g.shape[3]
     depth = g.shape[4]
+    chips = wide // 2
+    chip = w // 2
+    core = w % 2
     last = (((1,), (1,)), ((), ()))
-    for k in range(blocks):
-        q = jnp.concatenate([g[i, k].reshape(cols, depth) for i in range(wide)], axis=1)
+    first = (((0,), (0,)), ((), ()))
+    away = range(narrow - 1, -1, -1)
+
+    def products(k):
+        q = jnp.concatenate([g[k, i].reshape(cols, depth) for i in range(wide)], axis=1)
         plain = lax.dot_general(x[...], q, last, preferred_element_type=F32)
         rot_ref[k] = plain
         mapped = lax.dot_general(hx[...], q, last, preferred_element_type=F32)
         cor_ref[k] = ((mapped - plain * ritz_ref[k : k + 1, :]) * inv[k]).astype(BF16)
 
-    first = (((0,), (0,)), ((), ()))
-    chips = wide // 2
-    chip = w // 2
-    core = w % 2
-    for m in range(chips):
-        xc = x[:, 2 * m * depth : 2 * (m + 1) * depth]
-        for k in range(blocks):
+    def partials(k):
+        for m in range(chips):
+            xc = x[:, 2 * m * depth : 2 * (m + 1) * depth]
             part = lax.dot_general(cor_ref[k], xc, first, preferred_element_type=F32)
             for h in range(2):
                 half = part[:, h * depth : (h + 1) * depth].reshape(g.shape[2:])
-                p32[h, :, m, k] = half
-                p16[h, :, m, k] = half.astype(BF16)
-    away = range(narrow - 1, -1, -1)
-    for d in away:
-        push(p16.at[1 - core, flip(n, d)], r1.at[d], s1.at[d], t1.at[d], wide_to(CORE))
-    for d in away:
-        nd = flip(n, d)
-        arrived(r1.at[d], s1.at[d], t1.at[d], wide_to(CORE))
-        for i, m in enumerate(near):
-            j = flip(chip, m // 2)
-            a16[d, i] = (p32[core, nd, j] + r1[d, j].astype(F32)).astype(BF16)
-            push(a16.at[d, i], r2.at[d, i], s2.at[d, i], t2.at[d, i], wide_to(m))
+                p32[k, h, :, m] = half
+                p16[k, h, :, m] = half.astype(BF16)
+        for d in away:
+            push(p16.at[k, 1 - core, flip(n, d)], r1.at[k, d], s1.at[k, d], t1.at[k, d], wide_to(CORE))
+
+    def spread(k):
+        for d in away:
+            nd = flip(n, d)
+            arrived(r1.at[k, d], s1.at[k, d], t1.at[k, d], wide_to(CORE))
+            for i, m in enumerate(near):
+                j = flip(chip, m // 2)
+                a16[k, d, i] = (p32[k, core, nd, j] + r1[k, d, j].astype(F32)).astype(BF16)
+                push(a16.at[k, d, i], r2.at[k, d, i], s2.at[k, d, i], t2.at[k, d, i], wide_to(m))
+
+    pass_on(0)
+    gathered(0)
+    loads[3].wait()
+    loads[4].wait()
+    products(0)
+    for k in range(1, blocks):
+        pass_on(k)
+        partials(k - 1)
+        gathered(k)
+        products(k)
+        spread(k - 1)
+    partials(blocks - 1)
+    spread(blocks - 1)
+
     outs = []
     for i, (src, dst, dst_hbm) in enumerate(((rot_ref, rot_out, rot_hbm), (cor_ref, cor_out, cor_hbm))):
         dst[...] = jnp.stack([src[k].astype(F32) for k in range(blocks)], axis=1).astype(BF16)
         out = pltpu.make_async_copy(dst, dst_hbm, out_sem.at[i])
         out.start()
         outs.append(out)
-    for d in away:
-        total = p32[core, flip(n, d), chip] + r1[d, chip].astype(F32)
-        for i, m in enumerate(near):
-            arrived(r2.at[d, i], s2.at[d, i], t2.at[d, i], wide_to(m))
-            total = total + r2[d, i].astype(F32)
-        if d > 0:
-            f16[d] = total.astype(BF16)
-            push(f16.at[d], r4.at[d], s4.at[d], t4.at[d], narrow_to(d))
-    for d in away[:-1]:
-        arrived(r4.at[d], s4.at[d], t4.at[d], narrow_to(d))
-        total = total + r4[d].astype(F32)
-    mar_ref[...] = total * factor
+    for k in range(blocks):
+        for d in away:
+            total = p32[k, core, flip(n, d), chip] + r1[k, d, chip].astype(F32)
+            for i, m in enumerate(near):
+                arrived(r2.at[k, d, i], s2.at[k, d, i], t2.at[k, d, i], wide_to(m))
+                total = total + r2[k, d, i].astype(F32)
+            if d > 0:
+                f16[k, d] = total.astype(BF16)
+                push(f16.at[k, d], r4.at[k, d], s4.at[k, d], t4.at[k, d], narrow_to(d))
+        mar_ref[k] = total
+    for k in range(blocks):
+        total = mar_ref[k]
+        for d in away[:-1]:
+            arrived(r4.at[k, d], s4.at[k, d], t4.at[k, d], narrow_to(d))
+            total = total + r4[k, d].astype(F32)
+        mar_ref[k] = total * factor
     for out in outs:
         out.wait()
     for copy in sends:
@@ -198,7 +222,7 @@
     dma = pltpu.SemaphoreType.DMA
     vmem = pl.BlockSpec(memory_space=pltpu.VMEM)
     hbm = pl.BlockSpec(memory_space=pltpu.HBM)
-    tile = (narrow, part, depth)
+    unit = (part, depth)
     tile_in = (blocks, part, depth)
     chips = wide // 2
     rot, cor, mar = pl.pallas_call(
@@ -221,22 +245,22 @@
             pltpu.VMEM((1, rows), F32),
             pltpu.VMEM((rows, nst), BF16),
             pltpu.VMEM((rows, nst), BF16),
-            pltpu.VMEM((wide, blocks) + tile, BF16),
+            pltpu.VMEM((blocks, wide, narrow) + unit, BF16),
             pltpu.VMEM((blocks, rows, cols), F32),
-            pltpu.VMEM((2, narrow, chips) + tile_in, F32),
-            pltpu.VMEM((2, narrow, chips) + tile_in, BF16),
-            pltpu.VMEM((narrow, 3) + tile_in, BF16),
-            pltpu.VMEM((narrow, chips) + tile_in, BF16),
-            pltpu.VMEM((narrow, 3) + tile_in, BF16),
-            pltpu.VMEM((narrow,) + tile_in, BF16),
-            pltpu.VMEM((narrow,) + tile_in, BF16),
+            pltpu.VMEM((blocks, 2, narrow, chips) + unit, F32),
+            pltpu.VMEM((blocks, 2, narrow, chips) + unit, BF16),
+            pltpu.VMEM((blocks, narrow, 3) + unit, BF16),
+            pltpu.VMEM((blocks, narrow, chips) + unit, BF16),
+            pltpu.VMEM((blocks, narrow, 3) + unit, BF16),
+            pltpu.VMEM((blocks, narrow) + unit, BF16),
+            pltpu.VMEM((blocks, narrow) + unit, BF16),
             dma((5,)),
-            dma((narrow,)), dma((narrow,)),
-            dma((4, narrow)), dma((4, narrow)),
-            dma((3, narrow)), dma((3, narrow)),
-            dma((narrow,)), dma((narrow,)),
-            dma((narrow, 3)), dma((narrow, 3)),
-            dma((narrow,)), dma((narrow,)),
+            dma((blocks, narrow)), dma((blocks, narrow)),
+            dma((blocks, 4, narrow)), dma((blocks, 4, narrow)),
+            dma((blocks, 3, narrow)), dma((blocks, 3, narrow)),
+            dma((blocks, narrow)), dma((blocks, narrow)),
+            dma((blocks, narrow, 3)), dma((blocks, narrow, 3)),
+            dma((blocks, narrow)), dma((blocks, narrow)),
         ],
         compiler_params=pltpu.CompilerParams(
             collective_id=0, has_side_effects=True, vmem_limit_bytes=60 * 1024 * 1024),

time: 32.3 us -> 32.1 us (level)
  no operation moved by 1% of the time
where the time goes in v3:
time: 32.1 us; the launch traced here: 32 us
  Pallas kernels  31.3 us (98%)
  between operations  0.64 us (2%)
    pallas_call x1, Pallas kernels, fused(): pl.pallas_call(functools.partial(fused_kernel, factor, narrow), out_shape...  29.3 us
    pallas_call x1, Pallas kernels, hand_over(): pl.pallas_call(functools.partial(hand_over_kernel, cuts), out_shape=tuple...  2.01 us

profile of v3, /device:TPU:0, one launch (start us, length us, event | category | flops | bytes accessed | tf_op | source)
XLA Modules:
  0.0 32.0 jit_solution(1090859948449228430)
XLA Ops:
  0.6 29.3 %shard_map.76 = (bf16[512,2,256]{2,1,0:T(2,128)(2,1)}, bf16[512,2,256]{2,1,0:T(2,128)(2,1)}, f32[2,64,128]{2,1,0:T(8,128)}) custom-call(bf16[2,64,128]{2,1,0:T(8,128)(2,1)} %bitcast.3, f32[2,256]{1,0:T(2,128)} %ritz_hbm.1, f32[1,512]{1,0:T(1,128)} %bitcast.4, bf16[512,1024]{1,0:T(8,128)(2,1)} %x_hbm.1, bf16[512,1024]{1,0:T(8,128)(2,1)} %hx_hbm.1), custom_call_target="tpu_custom_call" | custom-call | tf_op jit(solution)/shard_map/pallas_call | solution.py:228
  29.9 2.0 %shard_map.77 = (bf16[512,2,256]{2,1,0:T(2,128)(2,1)}, bf16[512,2,256]{2,1,0:T(2,128)(2,1)}, f32[2,64,128]{2,1,0:T(8,128)}) custom-call(bf16[512,2,256]{2,1,0:T(2,128)(2,1)} %get-tuple-element.9.refs_0_, bf16[512,2,256]{2,1,0:T(2,128)(2,1)} %get-tuple-element.10.refs_1_, f32[2,64,128]{2,1,0:T(8,128)} %get-tuple-element.11.refs_2_), custom_call_target="tpu_custom_call" | custom-call | tf_op jit(solution)/shard_map/pallas_call | solution.py:206
